TPU v7x, 32 devices: a whole 2x2x4 slice. The times are simulated.
32 devices in a mesh: ka: 4 (over y, x), pw: 8 (over z, core).
Axes of the slice: x: 2, y: 2, z: 4, core: 2. Of those that a mesh axis runs over, the one named last changes fastest.
Arguments:
- band_coeffs: bfloat16 [4, 2, 1024, 384], P('ka', None, 'pw'), may hold values from -6 to 6
- cutoff_weight: float32 [4, 1024], P('ka', 'pw'), may hold values from 0.3 to 3
- row_order: int32 [4, 1024], P('ka', 'pw'), may hold values from 0 to 1023, as said below
- neighbour: int32 [4], P('ka'), may hold values from 0 to 3, as said below
- gauge_matrix: bfloat16 [4, 2, 384, 384], P('ka'), may hold values from -0.21875 to 0.21875
Outputs:
- whitened: bfloat16 [4, 2, 1024, 384], P('ka', None, 'pw')
- correlations: float32 [4, 2, 2, 384, 384], P('ka')
Inputs may be any that keep to these rules, and one draw needn't show every extreme that they name: `row_order`: within each aligned block of 128 entries of a row, the entries are a permutation of that block's own indices. neighbour[k] is (k + 1) mod 4 or (k - 1) mod 4; groups 0 and 1 take the second.
All inputs are finite; a program needn't handle non-finite values.
Results may differ from a plain program's by a relative error of at most 0.009.
Values may be sent and summed in bfloat16 or wider, within the bound.
A program may use at most 64 MiB of HBM per device.

v0:
```python
import math

import jax
import jax.numpy as jnp
from jax import lax
from jax.sharding import PartitionSpec as P

NB = 384
NS_STEPS = 2


def shifted(value, axis, steps):
    count = lax.axis_size(axis)
    pairs = [(source, (source + steps) % count) for source in range(count)]
    return lax.ppermute(value, axis, pairs)


def precise_dot(left, right):
    return jnp.dot(left, right, precision=lax.Precision.HIGHEST, preferred_element_type=jnp.float32)


def complex_product(left_re, left_im, right_re, right_im):
    real_part = precise_dot(left_re, right_re) - precise_dot(left_im, right_im)
    imag_part = precise_dot(left_re, right_im) + precise_dot(left_im, right_re)
    return (real_part, imag_part)


def lowered_dot(left, right):
    return jnp.dot(left, right, preferred_element_type=jnp.float32)


def whitening(gram_re, gram_im, scale):
    identity = jnp.eye(gram_re.shape[0], dtype=jnp.float32)
    upper_re = gram_re / scale
    upper_im = gram_im / scale
    lower_re = identity
    lower_im = jnp.zeros_like(identity)
    for ns_turn in range(NS_STEPS):
        prod_re, prod_im = complex_product(lower_re, lower_im, upper_re, upper_im)
        middle_re = 1.5 * identity - 0.5 * prod_re
        middle_im = -0.5 * prod_im
        upper_re, upper_im = complex_product(upper_re, upper_im, middle_re, middle_im)
        lower_re, lower_im = complex_product(middle_re, middle_im, lower_re, lower_im)
    return (lower_re, lower_im)


def cross_terms(whitened, moved_bands, local_order):
    moved = jnp.take(moved_bands, local_order, axis=1)
    cross = jnp.einsum("prn,qrm->pqnm", whitened, moved, preferred_element_type=jnp.float32)
    return (cross[0, 0] + cross[1, 1], cross[0, 1] - cross[1, 0])


def rotate(mix_re, mix_im, own_gauge, next_gauge):
    rot_re = (lowered_dot(mix_re, next_gauge[0]) - lowered_dot(mix_im, next_gauge[1])).astype(
        jnp.bfloat16
    )
    rot_im = (lowered_dot(mix_re, next_gauge[1]) + lowered_dot(mix_im, next_gauge[0])).astype(
        jnp.bfloat16
    )
    final_re = lowered_dot(own_gauge[0].T, rot_re) + lowered_dot(own_gauge[1].T, rot_im)
    final_im = lowered_dot(own_gauge[0].T, rot_im) - lowered_dot(own_gauge[1].T, rot_re)
    return jnp.stack([final_re, final_im])


def on_device(band_coeffs, cutoff_weight, row_order, neighbour, gauge_matrix):
    rows = band_coeffs.shape[2]
    pw_count = lax.axis_size("pw")
    pw_index = lax.axis_index("pw")
    root_scale = math.sqrt(rows * pw_count)
    filtered = (band_coeffs[0].astype(jnp.float32) * cutoff_weight[0][None, :, None]).astype(
        jnp.bfloat16
    )
    blocks = jnp.einsum("prn,qrm->pqnm", filtered, filtered, preferred_element_type=jnp.float32)
    local_re = blocks[0, 0] + blocks[1, 1]
    local_im = blocks[0, 1] - blocks[1, 0]
    gram_re, gram_im = lax.psum((local_re, local_im), "pw")
    squared = filtered.astype(jnp.float32)
    energy = lax.psum(jnp.sum(squared * squared), "pw")
    scale = 2.0 * energy / NB
    white_re, white_im = whitening(gram_re, gram_im, scale)
    wide_re = white_re.astype(jnp.bfloat16)
    wide_im = white_im.astype(jnp.bfloat16)
    out_re = lowered_dot(filtered[0], wide_re) - lowered_dot(filtered[1], wide_im)
    out_im = lowered_dot(filtered[0], wide_im) + lowered_dot(filtered[1], wide_re)
    whitened = jnp.stack([out_re, out_im]).astype(jnp.bfloat16)
    group_index = lax.axis_index("ka")
    group_count = lax.axis_size("ka")
    looks_ahead = neighbour[0] == (group_index + 1) % group_count
    ahead_pair = shifted((whitened, gauge_matrix[0]), "ka", -1)
    behind_pair = shifted((whitened, gauge_matrix[0]), "ka", 1)
    first_bands = jnp.where(looks_ahead, ahead_pair[0], behind_pair[0])
    second_bands = jnp.where(looks_ahead, behind_pair[0], ahead_pair[0])
    first_gauge = jnp.where(looks_ahead, ahead_pair[1], behind_pair[1])
    second_gauge = jnp.where(looks_ahead, behind_pair[1], ahead_pair[1])
    local_order = row_order[0] - pw_index * rows
    first_re, first_im = cross_terms(whitened, first_bands, local_order)
    second_re, second_im = cross_terms(whitened, second_bands, local_order)
    first_re, first_im, second_re, second_im = lax.psum(
        (first_re, first_im, second_re, second_im), "pw"
    )
    own_gauge = gauge_matrix[0]
    first_out = rotate(
        (first_re * root_scale).astype(jnp.bfloat16),
        (first_im * root_scale).astype(jnp.bfloat16),
        own_gauge,
        first_gauge,
    )
    second_out = rotate(
        (second_re * root_scale).astype(jnp.bfloat16),
        (second_im * root_scale).astype(jnp.bfloat16),
        own_gauge,
        second_gauge,
    )
    correlations = jnp.stack([first_out, second_out])
    return (whitened[None], correlations[None])


def solution(mesh):
    in_specs = (
        P("ka", None, "pw", None),
        P("ka", "pw"),
        P("ka", "pw"),
        P("ka"),
        P("ka", None, None, None),
    )
    out_specs = (P("ka", None, "pw", None), P("ka", None, None, None, None))
    return jax.shard_map(
        on_device, mesh=mesh, in_specs=in_specs, out_specs=out_specs, check_vma=False
    )
```

profile of v0, /device:TPU:0, one launch (start us, length us, event | category | flops | bytes accessed | tf_op | source)
XLA Modules:
  0.0 201.9 jit_solution(92365824114530461)
XLA Ops:
  7.2 1.6 convolution_bitcast_fusion.2
  11.5 19.0 %psum.50 = f32[]{:T(128)} all-reduce(f32[]{:T(128)} %get-tuple-element.15), channel_id=1, replica_groups=mesh['ka'=4,'pw'=8] {'pw'}, use_global_device_ids=true, to_apply=%region_2.0 | all-reduce | flops 1 | bytes 8 | tf_op jit(solution)/shard_map/psum | solution.py:78
  31.1 42.6 %all-reduce.7.cloned.1.call-done = (f32[384,384]{0,1:T(8,128)}, f32[384,384]{0,1:T(8,128)}) async-done(((f32[384,384]{0,1:T(8,128)}, f32[384,384]{0,1:T(8,128)}), (f32[384,384]{0,1:T(8,128)}, f32[384,384]{0,1:T(8,128)})) %all-reduce.7.cloned.1.call-update) | async-done | bytes 1179664 | tf_op jit(solution)/shard_map/psum | solution.py:76
  73.7 1.5 multiply_reduce_fusion
  75.2 1.7 fusion.9
  76.9 2.0 %fusion.82 = f32[384,384]{1,0:T(8,128)S(1)} fusion(f32[384,384]{0,1:T(8,128)S(1)} %fusion.9, f32[384,384]{0,1:T(8,128)S(1)} %copy-done.6, f32[]{:T(128)S(6)} %div.13), kind=kOutput, calls=%fused_computation.145 | convolution fusion | flops 679624704 | bytes 1769476 | tf_op jit(solution)/shard_map/dot_general | solution.py:19
  80.9 1.3 fusion.81
  82.9 1.3 convolution_subtract_fusion.2
  85.3 2.0 %convolution_add_fusion.3 = f32[384,384]{1,0:T(8,128)S(1)} fusion(f32[384,384]{1,0:T(8,128)S(1)} %fusion.81, f32[384,384]{0,1:T(8,128)S(1)} %fusion.9, f32[384,384]{0,1:T(8,128)S(1)} %copy-done.5, f32[]{:T(128)S(6)} %div.13), kind=kOutput, calls=%fused_computation.11 | convolution fusion | flops 679772160 | bytes 2359300 | tf_op jit(solution)/shard_map/dot_general | solution.py:19
  87.4 2.2 %convolution_add_fusion.4 = f32[384,384]{1,0:T(8,128)S(1)} fusion(f32[384,384]{1,0:T(8,128)S(1)} %fusion.26, f32[384,384]{0,1:T(8,128)S(1)} %fusion.9), kind=kOutput, calls=%fused_computation.12 | convolution fusion | flops 679624704 | bytes 1769472 | tf_op jit(solution)/shard_map/dot_general | solution.py:19
  89.6 1.3 fusion.84
  92.2 1.3 fusion.2
  93.6 1.3 fusion.85
  94.9 1.3 fusion.87
  101.1 2.4 %collective-permute-start = (bf16[2,128,384]{2,1,0:T(8,128)(2,1)S(1)}, bf16[2,128,384]{2,1,0:T(8,128)(2,1)S(1)}, u32[]{:S(2)}, u32[]{:S(2)}) collective-permute-start(bf16[2,128,384]{2,1,0:T(8,128)(2,1)S(1)} %pad_maximum_fusion.1), channel_id=1, source_target_pairs={{0,24},{8,0},{16,8},{24,16},{1,25},{9,1},{17,9},{25,17},{2,26},{10... | collective-permute-start | bytes 589832 | tf_op jit(solution)/shard_map/ppermute | solution.py:15
  104.3 3.9 %collective-permute-done = bf16[2,128,384]{2,1,0:T(8,128)(2,1)S(1)} collective-permute-done((bf16[2,128,384]{2,1,0:T(8,128)(2,1)S(1)}, bf16[2,128,384]{2,1,0:T(8,128)(2,1)S(1)}, u32[]{:S(2)}, u32[]{:S(2)}) %collective-permute-start) | collective-permute-done | bytes 196640 | tf_op jit(solution)/shard_map/ppermute | solution.py:15
  108.1 3.0 %collective-permute-done.1 = bf16[2,128,384]{2,1,0:T(8,128)(2,1)S(1)} collective-permute-done((bf16[2,128,384]{2,1,0:T(8,128)(2,1)S(1)}, bf16[2,128,384]{2,1,0:T(8,128)(2,1)S(1)}, u32[]{:S(2)}, u32[]{:S(2)}) %collective-permute-start.1) | collective-permute-done | bytes 196640 | tf_op jit(solution)/shard_map/ppermute | solution.py:15
  118.3 1.5 collective-permute-start.2
  121.0 13.5 %collective-permute-done.2 = bf16[2,384,384]{2,1,0:T(8,128)(2,1)S(1)} collective-permute-done((bf16[2,384,384]{2,1,0:T(8,128)(2,1)S(1)}, bf16[2,384,384]{2,1,0:T(8,128)(2,1)S(1)}, u32[]{:S(2)}, u32[]{:S(2)}) %collective-permute-start.2) | collective-permute-done | bytes 589856 | tf_op jit(solution)/shard_map/ppermute | solution.py:15
  134.5 8.6 %collective-permute-done.3 = bf16[2,384,384]{2,1,0:T(8,128)(2,1)S(1)} collective-permute-done((bf16[2,384,384]{2,1,0:T(8,128)(2,1)S(1)}, bf16[2,384,384]{2,1,0:T(8,128)(2,1)S(1)}, u32[]{:S(2)}, u32[]{:S(2)}) %collective-permute-start.3) | collective-permute-done | bytes 589856 | tf_op jit(solution)/shard_map/ppermute | solution.py:15
  143.2 41.2 %all-reduce.5.cloned.1.call-done = (f32[384,384]{0,1:T(8,128)}, f32[384,384]{0,1:T(8,128)}, f32[384,384]{0,1:T(8,128)}, f32[384,384]{0,1:T(8,128)}) async-done(((f32[384,384]{0,1:T(8,128)}, f32[384,384]{0,1:T(8,128)}, f32[384,384]{0,1:T(8,128)}, f32[384,384]{0,1:T(8,128)}), (f32[384,384]{0,1:T(8,128)}, f32[384,384]{0,1:T(8,128)}, f32[384,384]{0,1:T(8,128)}, ...) | async-done | bytes 2359312 | tf_op jit(solution)/shard_map/psum | solution.py:98
  184.4 1.5 fusion.48
  185.9 1.5 fusion.47
  193.1 2.0 copy.32
  (73 shorter events, 26.5 us)
Async XLA Ops:
  7.2 66.6 %all-reduce.7.cloned.1.call-start = ((), (), s32[]{:S(2)}) async-start(), calls=%async_computation.1 | async-start | bytes 2359296 | tf_op jit(solution)/shard_map/psum | solution.py:76
  8.8 1.9 copy-start.4
  8.9 1.9 copy-start.7
  10.7 173.7 %all-reduce.5.cloned.1.call-start = ((), (), s32[]{:S(2)}) async-start(), calls=%async_computation | async-start | bytes 4718592 | tf_op jit(solution)/shard_map/psum | solution.py:98
  73.7 3.2 %copy-start.6 = (f32[384,384]{0,1:T(8,128)S(1)}, f32[384,384]{0,1:T(8,128)}, u32[]{:S(2)}) copy-start(f32[384,384]{0,1:T(8,128)} %get-tuple-element.12) | copy-start | bytes 1769476
  76.9 3.2 %copy-start.5 = (f32[384,384]{0,1:T(8,128)S(1)}, f32[384,384]{0,1:T(8,128)}, u32[]{:S(2)}) copy-start(f32[384,384]{0,1:T(8,128)} %get-tuple-element.11) | copy-start | bytes 1769476
  98.7 4.8 %copy-start.8 = (s32[1,128]{1,0:T(1,128)S(1)}, s32[1,128]{1,0:T(1,128)}, u32[]{:S(2)}) copy-start(s32[1,128]{1,0:T(1,128)} %param.9) | copy-start | bytes 1540
  101.1 7.0 %collective-permute-start = (bf16[2,128,384]{2,1,0:T(8,128)(2,1)S(1)}, bf16[2,128,384]{2,1,0:T(8,128)(2,1)S(1)}, u32[]{:S(2)}, u32[]{:S(2)}) collective-permute-start(bf16[2,128,384]{2,1,0:T(8,128)(2,1)S(1)} %pad_maximum_fusion.1), channel_id=1, source_target_pairs={{0,24},{8,0},{16,8},{24,16},{1,25},{9,1},{17,9},{25,17},{2,26},{10... | collective-permute-start | bytes 589832 | tf_op jit(solution)/shard_map/ppermute | solution.py:15
  103.6 7.6 %collective-permute-start.1 = (bf16[2,128,384]{2,1,0:T(8,128)(2,1)S(1)}, bf16[2,128,384]{2,1,0:T(8,128)(2,1)S(1)}, u32[]{:S(2)}, u32[]{:S(2)}) collective-permute-start(bf16[2,128,384]{2,1,0:T(8,128)(2,1)S(1)} %pad_maximum_fusion.1), channel_id=1, source_target_pairs={{0,8},{8,16},{16,24},{24,0},{1,9},{9,17},{17,25},{25,1},{2,10},{10... | collective-permute-start | bytes 589832 | tf_op jit(solution)/shard_map/ppermute | solution.py:15
  117.1 1.2 copy-start
  118.3 16.3 %collective-permute-start.2 = (bf16[2,384,384]{2,1,0:T(8,128)(2,1)S(1)}, bf16[2,384,384]{2,1,0:T(8,128)(2,1)S(1)}, u32[]{:S(2)}, u32[]{:S(2)}) collective-permute-start(bf16[2,384,384]{2,1,0:T(8,128)(2,1)S(1)} %bitcast.182), channel_id=1, source_target_pairs={{0,24},{8,0},{16,8},{24,16},{1,25},{9,1},{17,9},{25,17},{2,26},{10... | collective-permute-start | bytes 1769480 | tf_op jit(solution)/shard_map/ppermute | solution.py:15
  119.8 23.3 %collective-permute-start.3 = (bf16[2,384,384]{2,1,0:T(8,128)(2,1)S(1)}, bf16[2,384,384]{2,1,0:T(8,128)(2,1)S(1)}, u32[]{:S(2)}, u32[]{:S(2)}) collective-permute-start(bf16[2,384,384]{2,1,0:T(8,128)(2,1)S(1)} %bitcast.183), channel_id=1, source_target_pairs={{0,8},{8,16},{16,24},{24,0},{1,9},{9,17},{17,25},{25,1},{2,10},{10... | collective-permute-start | bytes 1769480 | tf_op jit(solution)/shard_map/ppermute | solution.py:15
  184.4 3.0 %copy-start.3 = (f32[384,384]{0,1:T(8,128)S(1)}, f32[384,384]{0,1:T(8,128)}, u32[]{:S(2)}) copy-start(f32[384,384]{0,1:T(8,128)} %get-tuple-element.7) | copy-start | bytes 1769476
  185.9 2.3 %copy-start.2 = (f32[384,384]{0,1:T(8,128)S(1)}, f32[384,384]{0,1:T(8,128)}, u32[]{:S(2)}) copy-start(f32[384,384]{0,1:T(8,128)} %get-tuple-element.10) | copy-start | bytes 1769476
  189.3 1.1 copy-start.1
Sparse Core Ops, SparseCore 0:
  10.9 62.7 all-reduce.6
  118.4 65.9 all-reduce.4
where the time goes:
time: 202 us
  waiting for transfers between devices  113 us (56%)
  matrix products  36.5 us (18%)
  blocking collectives  19 us (9%)
  between operations  15.9 us (8%)
  other arithmetic  8.57 us (4%)
  local copies, waits for them, and re-layouts  4.69 us (2%)
  starting transfers between devices  4.58 us (2%)
    psum x1, waiting for transfers between devices, on_device(): gram_re, gram_im = lax.psum((local_re, local_im), 'pw')  42.6 us
    psum x1, waiting for transfers between devices, on_device(): lax.psum((first_re, first_im, second_re, second_im), 'pw')  41.2 us
    ppermute x4, waiting for transfers between devices, shifted(): return lax.ppermute(value, axis, pairs)  29 us
    dot_general x18, matrix products, precise_dot(): jnp.dot(left, right, precision=lax.Precision.HIGHEST, preferred_element_t...  24.6 us
    psum x1, blocking collectives, on_device(): energy = lax.psum(jnp.sum(squared * squared), 'pw')  19 us
    dot_general x20, matrix products, lowered_dot(): return jnp.dot(left, right, preferred_element_type=jnp.float32)  9.31 us
    ppermute x4, starting transfers between devices, shifted(): return lax.ppermute(value, axis, pairs)  4.5 us
  transfers between devices with their start and end apart: 6, of which 6 were waited for; matrix products, arithmetic and copies ran while one was open for 1% of the time, Pallas kernels for 0%

commit v1 on v0

v1 whole, which is shorter than its diff:
```python
import functools
import math

import jax
import jax.numpy as jnp
from jax import lax
from jax.experimental import pallas as pl
from jax.experimental.pallas import tpu as pltpu
from jax.sharding import PartitionSpec as P

MESH = pl.DeviceIdType.MESH
CORES = 2
A_CHUNKS = 4
F32 = jnp.float32
BF16 = jnp.bfloat16


def mm(left, right):
    return jnp.dot(left, right, preferred_element_type=F32)


def mm_t(left, right):
    return lax.dot_general(left, right, (((0,), (0,)), ((), ())), preferred_element_type=F32)


def complex_mm(left_re, left_im, right_re, right_im):
    real_part = mm(left_re, right_re) - mm(left_im, right_im)
    imag_part = mm(left_re, right_im) + mm(left_im, right_re)
    return real_part, imag_part


def halves(packed):
    turned = packed.T
    return 0.5 * (packed + turned), 0.5 * (packed - turned)


def kernel(
    ka_count,
    pw_count,
    bands_ref,
    weight_ref,
    order_ref,
    gauge_ref,
    white_out,
    corr_out,
    f_buf,
    p_buf,
    fn_buf,
    un_buf,
    a_full,
    local,
    r_buf,
    l_buf,
    s_buf,
    t_buf,
    a_other,
    w_buf,
    wn_buf,
    v_buf,
    c_buf,
    pair_send,
    pair_recv,
    near_send,
    fn_recv,
    un_recv,
    wn_recv,
    red_send,
    red_recv_r,
    red_recv_l,
    tot_recv,
    cast_send,
):
    rows, nb = bands_ref.shape[1], bands_ref.shape[2]
    half = nb // CORES
    chunk = half // A_CHUNKS
    c_chunks = nb // chunk
    pairs_a = A_CHUNKS // 2
    pairs_all = (A_CHUNKS + 2 * c_chunks) // 2
    k = lax.axis_index("ka")
    p = lax.axis_index("pw")
    core = lax.rem(p, CORES)
    q = lax.div(p, CORES)
    line = pw_count // CORES
    low = (line - 1) // 2
    ahead = lax.rem(k + 1, ka_count)
    behind = lax.rem(k + ka_count - 1, ka_count)
    base = q * CORES
    partner = base + 1 - core

    barrier = pltpu.get_barrier_semaphore()

    def greet(a, b):
        pl.semaphore_signal(barrier, inc=1, device_id=(a, b), device_id_type=MESH)

    greet(k, partner)
    for other in (ahead, behind):
        for side in range(CORES):
            greet(other, base + side)

    @pl.when(q > 0)
    def _():
        greet(k, p - CORES)

    @pl.when(q < line - 1)
    def _():
        greet(k, p + CORES)

    row_id = lax.broadcasted_iota(jnp.int32, (rows, rows), 0)
    col_id = lax.broadcasted_iota(jnp.int32, (rows, rows), 1)
    weight = jnp.sum(jnp.where(row_id == col_id, weight_ref[...], 0.0), axis=1, keepdims=True)
    pick = (row_id == order_ref[...] - p * rows).astype(BF16)
    for part in range(2):
        filtered = (bands_ref[part].astype(F32) * weight).astype(BF16)
        f_buf[part] = filtered
        p_buf[core, part] = mm(pick, filtered).astype(BF16)

    @pl.when(q == 0)
    def _():
        r_buf[...] = jnp.zeros_like(r_buf)

    @pl.when(q == line - 1)
    def _():
        l_buf[...] = jnp.zeros_like(l_buf)

    pl.semaphore_wait(barrier, 5 + (q > 0).astype(jnp.int32) + (q < line - 1).astype(jnp.int32))

    def remote(src, dst, send, recv, a, b):
        return pltpu.make_async_remote_copy(
            src_ref=src, dst_ref=dst, send_sem=send, recv_sem=recv,
            device_id=(a, b), device_id_type=MESH,
        )

    def to_pair(src, dst, turn):
        return remote(src, dst, pair_send.at[turn], pair_recv.at[turn], k, partner)

    def to_near(src, dst, recv, turn):
        return (
            remote(src, dst, near_send.at[turn, 0], recv, behind, base),
            remote(src, dst, near_send.at[turn, 1], recv, ahead, base + 1),
        )

    def from_near(buf, recv, turn):
        for side in range(CORES):
            remote(buf.at[side], buf.at[side], near_send.at[turn, 0], recv.at[side], k, partner).wait_recv()

    p_copy = to_pair(p_buf.at[core], p_buf.at[core], 0)
    p_copy.start()
    f_copies = to_near(f_buf, fn_buf.at[core], fn_recv.at[core], 0)
    u_copies = to_near(gauge_ref.at[core], un_buf.at[core], un_recv.at[core], 1)
    for copy in f_copies + u_copies:
        copy.start()

    def got_pair(dst, turn):
        remote(dst, dst, pair_send.at[turn], pair_recv.at[turn], k, partner).wait_recv()

    got_pair(p_buf.at[1 - core], 0)

    def stacked(buf):
        flat = buf[...].reshape(CORES * 2 * rows, nb)
        turned = []
        for side in range(CORES):
            turned += [buf[side, 1], -buf[side, 0]]
        return flat, jnp.concatenate(turned, axis=0)

    own_flat, own_turned = stacked(p_buf)
    a_full[...] = mm_t(own_flat, own_flat) + mm_t(own_flat, own_turned)
    for i in range(A_CHUNKS):
        local[i] = a_full[pl.ds(pl.multiple_of(core * half + i * chunk, 8), chunk), :]

    def reduce_one(i):
        owner = low + lax.rem(i, 2) if line > 1 else 0

        @pl.when(q < owner)
        def _():
            @pl.when(q > 0)
            def _():
                remote(r_buf.at[i], r_buf.at[i], red_send.at[i], red_recv_r.at[i], k, partner).wait_recv()

            s_buf[i] = (local[i] + r_buf[i].astype(F32)).astype(BF16)
            remote(s_buf.at[i], r_buf.at[i], red_send.at[i], red_recv_r.at[i], k, p + CORES).start()

        @pl.when(q > owner)
        def _():
            @pl.when(q < line - 1)
            def _():
                remote(l_buf.at[i], l_buf.at[i], red_send.at[i], red_recv_l.at[i], k, partner).wait_recv()

            s_buf[i] = (local[i] + l_buf[i].astype(F32)).astype(BF16)
            remote(s_buf.at[i], l_buf.at[i], red_send.at[i], red_recv_l.at[i], k, p - CORES).start()

        @pl.when(q == owner)
        def _():
            @pl.when(q > 0)
            def _():
                remote(r_buf.at[i], r_buf.at[i], red_send.at[i], red_recv_r.at[i], k, partner).wait_recv()

            @pl.when(q < line - 1)
            def _():
                remote(l_buf.at[i], l_buf.at[i], red_send.at[i], red_recv_l.at[i], k, partner).wait_recv()

            t_buf[i] = (local[i] + r_buf[i].astype(F32) + l_buf[i].astype(F32)).astype(BF16)

            @pl.when(q > 0)
            def _():
                remote(t_buf.at[i], t_buf.at[i], cast_send.at[0, i], tot_recv.at[i], k, p - CORES).start()

            @pl.when(q < line - 1)
            def _():
                remote(t_buf.at[i], t_buf.at[i], cast_send.at[1, i], tot_recv.at[i], k, p + CORES).start()

    def cast_one(i):
        owner = low + lax.rem(i, 2) if line > 1 else 0

        @pl.when(q != owner)
        def _():
            remote(t_buf.at[i], t_buf.at[i], cast_send.at[0, i], tot_recv.at[i], k, partner).wait_recv()

        @pl.when((q < owner) & (q > 0))
        def _():
            remote(t_buf.at[i], t_buf.at[i], cast_send.at[0, i], tot_recv.at[i], k, p - CORES).start()

        @pl.when((q > owner) & (q < line - 1))
        def _():
            remote(t_buf.at[i], t_buf.at[i], cast_send.at[1, i], tot_recv.at[i], k, p + CORES).start()

    def settle_one(i):
        owner = low + lax.rem(i, 2) if line > 1 else 0

        @pl.when(q != owner)
        def _():
            remote(s_buf.at[i], s_buf.at[i], red_send.at[i], tot_recv.at[i], k, partner).wait_send()

        @pl.when((q <= owner) & (q > 0))
        def _():
            remote(t_buf.at[i], t_buf.at[i], cast_send.at[0, i], tot_recv.at[i], k, partner).wait_send()

        @pl.when((q >= owner) & (q < line - 1))
        def _():
            remote(t_buf.at[i], t_buf.at[i], cast_send.at[1, i], tot_recv.at[i], k, partner).wait_send()

    at_low = (q <= low).astype(jnp.int32)

    def over_pairs(one, first, last):
        def step(j, carry):
            one(2 * j + at_low)
            one(2 * j + 1 - at_low)
            return carry

        lax.fori_loop(first, last, step, 0)

    over_pairs(reduce_one, 0, pairs_a)
    over_pairs(cast_one, 0, pairs_a)

    mine = pl.ds(0, A_CHUNKS)
    a_copy = to_pair(t_buf.at[mine], a_other, 1)
    a_copy.start()

    from_near(fn_buf, fn_recv, 0)
    near_flat, near_turned = stacked(fn_buf)
    local[A_CHUNKS : A_CHUNKS + c_chunks] = mm_t(own_flat, near_flat).reshape(c_chunks, chunk, nb)
    local[A_CHUNKS + c_chunks :] = mm_t(own_flat, near_turned).reshape(c_chunks, chunk, nb)

    outer = (q == 0) | (q == line - 1)

    @pl.when(outer)
    def _():
        over_pairs(reduce_one, pairs_a, pairs_all)

    got_pair(a_other, 1)
    a_full[pl.ds(pl.multiple_of(core * half, 8), half), :] = (
        t_buf[mine].astype(F32).reshape(half, nb)
    )
    a_full[pl.ds(pl.multiple_of((1 - core) * half, 8), half), :] = (
        a_other[...].astype(F32).reshape(half, nb)
    )

    eye = (
        lax.broadcasted_iota(jnp.int32, (nb, nb), 0) == lax.broadcasted_iota(jnp.int32, (nb, nb), 1)
    ).astype(F32)
    packed = a_full[...]
    scale = 2.0 * jnp.sum(packed * eye) / nb
    y_re, y_im = halves(packed / scale)
    y_re_b, y_im_b = y_re.astype(BF16), y_im.astype(BF16)
    sq_re, sq_im = complex_mm(y_re_b, y_im_b, y_re_b, y_im_b)
    left_re = (1.5 * y_re - 0.5 * sq_re).astype(BF16)
    left_im = (1.5 * y_im - 0.5 * sq_im).astype(BF16)
    right_re = (2.25 * eye - 1.5 * y_re + 0.25 * sq_re).astype(BF16)
    right_im = (0.25 * sq_im - 1.5 * y_im).astype(BF16)
    last_re, last_im = complex_mm(left_re, left_im, right_re, right_im)
    white_re = 2.25 * eye - 0.75 * y_re - 0.5 * last_re
    white_im = -0.75 * y_im - 0.5 * last_im
    w_buf[...] = (white_re + white_im).astype(BF16).reshape(CORES, half, nb)
    w_copies = to_near(w_buf.at[core], wn_buf.at[core], wn_recv.at[core], 2)
    for copy in w_copies:
        copy.start()
    w_re, w_im = white_re.astype(BF16), white_im.astype(BF16)

    @pl.when(jnp.logical_not(outer))
    def _():
        over_pairs(reduce_one, pairs_a, pairs_all)

    out_re, out_im = complex_mm(f_buf[0], f_buf[1], w_re, w_im)
    white_out[0] = out_re.astype(BF16)
    white_out[1] = out_im.astype(BF16)
    v_re, v_im = complex_mm(w_re, w_im, gauge_ref[0], gauge_ref[1])
    v_buf[0] = v_re.astype(BF16)
    v_buf[1] = v_im.astype(BF16)

    over_pairs(cast_one, pairs_a, pairs_all)
    from_near(un_buf, un_recv, 1)
    from_near(wn_buf, wn_recv, 2)
    next_re, next_im = halves(wn_buf[...].astype(F32).reshape(nb, nb))
    vn_re, vn_im = complex_mm(next_re.astype(BF16), next_im.astype(BF16), un_buf[0], un_buf[1])
    cross_re = t_buf[A_CHUNKS : A_CHUNKS + c_chunks].reshape(nb, nb)
    cross_im = t_buf[A_CHUNKS + c_chunks :].reshape(nb, nb)
    x_re, x_im = complex_mm(cross_re, cross_im, vn_re.astype(BF16), vn_im.astype(BF16))
    x_re, x_im = x_re.astype(BF16), x_im.astype(BF16)
    root = math.sqrt(rows * pw_count)
    corr_re = mm_t(v_buf[0], x_re) + mm_t(v_buf[1], x_im)
    corr_im = mm_t(v_buf[0], x_im) - mm_t(v_buf[1], x_re)
    c_buf[core, 0] = (corr_re * root).astype(BF16)
    c_buf[core, 1] = (corr_im * root).astype(BF16)
    c_copy = to_pair(c_buf.at[core], c_buf.at[core], 2)
    c_copy.start()

    for copy in (p_copy, a_copy) + f_copies + u_copies + w_copies:
        copy.wait_send()

    def settle(i, carry):
        settle_one(i)
        return carry

    lax.fori_loop(0, 2 * pairs_all, settle, 0)
    got_pair(c_buf.at[1 - core], 2)
    corr_out[...] = c_buf[...]
    c_copy.wait_send()


def on_device(ka_count, pw_count, band_coeffs, cutoff_weight, row_order, neighbour, gauge_matrix):
    rows, nb = band_coeffs.shape[2], band_coeffs.shape[3]
    half = nb // CORES
    chunk = half // A_CHUNKS
    total = A_CHUNKS + 2 * (nb // chunk)
    vmem = pl.BlockSpec(memory_space=pltpu.VMEM)
    dma = pltpu.SemaphoreType.DMA
    whitened, pair = pl.pallas_call(
        functools.partial(kernel, ka_count, pw_count),
        out_shape=(
            jax.ShapeDtypeStruct((2, rows, nb), BF16),
            jax.ShapeDtypeStruct((2, 2, nb, nb), BF16),
        ),
        in_specs=[vmem] * 4,
        out_specs=(vmem, vmem),
        scratch_shapes=[
            pltpu.VMEM((2, rows, nb), BF16),
            pltpu.VMEM((CORES, 2, rows, nb), BF16),
            pltpu.VMEM((CORES, 2, rows, nb), BF16),
            pltpu.VMEM((2, nb, nb), BF16),
            pltpu.VMEM((nb, nb), F32),
            pltpu.VMEM((total, chunk, nb), F32),
            pltpu.VMEM((total, chunk, nb), BF16),
            pltpu.VMEM((total, chunk, nb), BF16),
            pltpu.VMEM((total, chunk, nb), BF16),
            pltpu.VMEM((total, chunk, nb), BF16),
            pltpu.VMEM((A_CHUNKS, chunk, nb), BF16),
            pltpu.VMEM((CORES, half, nb), BF16),
            pltpu.VMEM((CORES, half, nb), BF16),
            pltpu.VMEM((2, nb, nb), BF16),
            pltpu.VMEM((2, 2, nb, nb), BF16),
            dma((3,)),
            dma((3,)),
            dma((3, 2)),
            dma((2,)),
            dma((2,)),
            dma((2,)),
            dma((total,)),
            dma((total,)),
            dma((total,)),
            dma((total,)),
            dma((2, total)),
        ],
        compiler_params=pltpu.CompilerParams(collective_id=0, has_side_effects=True),
    )(band_coeffs[0], cutoff_weight, row_order, gauge_matrix[0])
    group = lax.axis_index("ka")
    looks_ahead = neighbour[0] == (group + 1) % ka_count
    correlations = jnp.where(looks_ahead, pair, pair[::-1]).astype(F32)
    return (whitened[None], correlations[None])


def solution(mesh):
    in_specs = (
        P("ka", None, "pw", None),
        P("ka", "pw"),
        P("ka", "pw"),
        P("ka"),
        P("ka", None, None, None),
    )
    out_specs = (P("ka", None, "pw", None), P("ka", None, None, None, None))
    return jax.shard_map(
        functools.partial(on_device, mesh.shape["ka"], mesh.shape["pw"]),
        mesh=mesh, in_specs=in_specs, out_specs=out_specs, check_vma=False,
    )
```

time: 202 us -> 74.6 us (0.37)
  waiting for transfers between devices: 113 us -> 0 us
  Pallas kernels: 0 us -> 69.1 us
  matrix products: 36.5 us -> 0 us
  blocking collectives: 19 us -> 0 us
  between operations: 15.9 us -> 1.31 us
  other arithmetic: 8.57 us -> 3.3 us
  starting transfers between devices: 4.58 us -> 0 us
  local copies, waits for them, and re-layouts: 4.69 us -> 0.68 us
    psum x2 -> x0, waiting for transfers between devices: 83.7 us -> none  [the longest x1 42.6 us: on_device(): gram_re, gram_im = lax.psum((local_re, local_im), 'pw')]
    pallas_call x0 -> x1, Pallas kernels: none -> 69.1 us  [on_device(): pl.pallas_call(functools.partial(kernel, ka_count, pw_count), out_shape=(...]
    dot_general x41 -> x0, matrix products: 36.5 us -> none  [the longest x18 24.6 us: precise_dot(): jnp.dot(left, right, precision=lax.Precision.HIGHEST, preferred_element_t...]
    ppermute x4 -> x0, waiting for transfers between devices: 29 us -> none  [shifted(): return lax.ppermute(value, axis, pairs)]
    psum x1 -> x0, blocking collectives: 19 us -> none  [on_device(): energy = lax.psum(jnp.sum(squared * squared), 'pw')]
    ppermute x4 -> x0, starting transfers between devices: 4.5 us -> none  [shifted(): return lax.ppermute(value, axis, pairs)]
    broadcast_in_dim x1, other arithmetic: 0.15 us -> 3.3 us  [on_device(): return (whitened[None], correlations[None])]
    add x3 -> x0, other arithmetic: 2.9 us -> none  [the longest x2 2.01 us: cross_terms(): return (cross[0, 0] + cross[1, 1], cross[0, 1] - cross[1, 0])]
  transfers between devices with their start and end apart: 6 -> 0, of which waited for: 6 -> 0; matrix products, arithmetic and copies ran while one was open for 1% -> 0% of each run, Pallas kernels for 0% -> 0%
where the time goes in v1:
time: 74.6 us; the launch traced here: 74.4 us
  Pallas kernels  69.1 us (93%)
  other arithmetic  3.3 us (4%)
  between operations  1.31 us (2%)
    pallas_call x1, Pallas kernels, on_device(): pl.pallas_call(functools.partial(kernel, ka_count, pw_count), out_shape=(...  69.1 us
    broadcast_in_dim x1, other arithmetic, on_device(): return (whitened[None], correlations[None])  3.3 us

profile of v1, /device:TPU:0, one launch (start us, length us, event | category | flops | bytes accessed | tf_op | source)
XLA Modules:
  0.0 74.4 jit_solution(9742034694354023819)
XLA Ops:
  1.3 69.1 %shard_map.68 = (bf16[2,128,384]{2,1,0:T(8,128)(2,1)}, bf16[2,2,384,384]{3,2,1,0:T(8,128)(2,1)}) custom-call(bf16[2,128,384]{2,1,0:T(8,128)(2,1)} %bitcast.12, f32[1,128]{1,0:T(1,128)} %weight_ref.1, s32[1,128]{1,0:T(1,128)} %order_ref.1, bf16[2,384,384]{2,1,0:T(8,128)(2,1)} %bitcast.10), custom_call_target="tpu_custom_call" | custom-call | tf_op jit(solution)/shard_map/pallas_call | solution.py:346
  70.4 0.0 copy-start
  70.5 3.3 %fusion.1 = f32[1,2,2,384,384]{4,3,2,1,0:T(8,128)} fusion(bf16[2,2,384,384]{3,2,1,0:T(8,128)(2,1)} %get-tuple-element.5, pred[]{:T(512)S(6)} %eq.5), kind=kLoop, calls=%fused_computation.2 | loop fusion | flops 1179648 | bytes 3538945 | tf_op jit(solution)/shard_map/broadcast_in_dim | solution.py:387
  73.8 0.0 copy-done
  73.8 0.7 copy.9
Async XLA Ops:
  70.4 3.3 %copy-start = (bf16[2,128,384]{2,1,0:T(8,128)(2,1)S(1)}, bf16[2,128,384]{2,1,0:T(8,128)(2,1)}, u32[]{:S(2)}) copy-start(bf16[2,128,384]{2,1,0:T(8,128)(2,1)} %get-tuple-element.4) | copy-start | bytes 589828

commit v2 on v1

--- a/solution.py
+++ b/solution.py
@@ -11,6 +11,9 @@
 MESH = pl.DeviceIdType.MESH
 CORES = 2
 A_CHUNKS = 4
+EARLY = 1
+TOTAL_LAG = 3
+CAST_LAG = 6
 F32 = jnp.float32
 BF16 = jnp.bfloat16
 
@@ -76,6 +79,7 @@
     c_chunks = nb // chunk
     pairs_a = A_CHUNKS // 2
     pairs_all = (A_CHUNKS + 2 * c_chunks) // 2
+    early = pairs_a + EARLY
     k = lax.axis_index("ka")
     p = lax.axis_index("pw")
     core = lax.rem(p, CORES)
@@ -147,7 +151,7 @@
     p_copy.start()
     f_copies = to_near(f_buf, fn_buf.at[core], fn_recv.at[core], 0)
     u_copies = to_near(gauge_ref.at[core], un_buf.at[core], un_recv.at[core], 1)
-    for copy in f_copies + u_copies:
+    for copy in f_copies:
         copy.start()
 
     def got_pair(dst, turn):
@@ -167,7 +171,7 @@
     for i in range(A_CHUNKS):
         local[i] = a_full[pl.ds(pl.multiple_of(core * half + i * chunk, 8), chunk), :]
 
-    def reduce_one(i):
+    def relay_one(i):
         owner = low + lax.rem(i, 2) if line > 1 else 0
 
         @pl.when(q < owner)
@@ -188,6 +192,9 @@
             s_buf[i] = (local[i] + l_buf[i].astype(F32)).astype(BF16)
             remote(s_buf.at[i], l_buf.at[i], red_send.at[i], red_recv_l.at[i], k, p - CORES).start()
 
+    def total_one(i):
+        owner = low + lax.rem(i, 2) if line > 1 else 0
+
         @pl.when(q == owner)
         def _():
             @pl.when(q > 0)
@@ -238,34 +245,61 @@
         def _():
             remote(t_buf.at[i], t_buf.at[i], cast_send.at[1, i], tot_recv.at[i], k, partner).wait_send()
 
-    at_low = (q <= low).astype(jnp.int32)
-
     def over_pairs(one, first, last):
-        def step(j, carry):
-            one(2 * j + at_low)
-            one(2 * j + 1 - at_low)
+        def step(i, carry):
+            one(i)
             return carry
 
-        lax.fori_loop(first, last, step, 0)
-
-    over_pairs(reduce_one, 0, pairs_a)
+        lax.fori_loop(2 * first, 2 * last, step, 0)
+
+    outer = (q == 0) | (q == line - 1)
+    inner = jnp.logical_not(outer)
+
+    def cross_terms():
+        from_near(fn_buf, fn_recv, 0)
+        near_flat, near_turned = stacked(fn_buf)
+        for part, right in enumerate((near_flat, near_turned)):
+            cross = mm_t(own_flat, right)
+            for j in range(c_chunks):
+                local[A_CHUNKS + 2 * j + part] = cross[j * chunk : (j + 1) * chunk]
+
+    over_pairs(relay_one, 0, pairs_a)
+    over_pairs(total_one, 0, pairs_a)
+
+    @pl.when(outer)
+    def _():
+        cross_terms()
+        over_pairs(relay_one, pairs_a, pairs_all)
+
     over_pairs(cast_one, 0, pairs_a)
 
     mine = pl.ds(0, A_CHUNKS)
     a_copy = to_pair(t_buf.at[mine], a_other, 1)
     a_copy.start()
 
-    from_near(fn_buf, fn_recv, 0)
-    near_flat, near_turned = stacked(fn_buf)
-    local[A_CHUNKS : A_CHUNKS + c_chunks] = mm_t(own_flat, near_flat).reshape(c_chunks, chunk, nb)
-    local[A_CHUNKS + c_chunks :] = mm_t(own_flat, near_turned).reshape(c_chunks, chunk, nb)
-
-    outer = (q == 0) | (q == line - 1)
-
-    @pl.when(outer)
-    def _():
-        over_pairs(reduce_one, pairs_a, pairs_all)
-
+    @pl.when(inner)
+    def _():
+        cross_terms()
+
+    for copy in u_copies:
+        copy.start()
+
+    def sums(j, carry):
+        @pl.when(inner & (j < pairs_all))
+        def _():
+            over_pairs(relay_one, j, j + 1)
+
+        @pl.when((j >= pairs_a + TOTAL_LAG) & (j < pairs_all + TOTAL_LAG))
+        def _():
+            over_pairs(total_one, j - TOTAL_LAG, j - TOTAL_LAG + 1)
+
+        @pl.when(j >= pairs_a + CAST_LAG)
+        def _():
+            over_pairs(cast_one, j - CAST_LAG, j - CAST_LAG + 1)
+
+        return carry
+
+    lax.fori_loop(pairs_a, early, sums, 0)
     got_pair(a_other, 1)
     a_full[pl.ds(pl.multiple_of(core * half, 8), half), :] = (
         t_buf[mine].astype(F32).reshape(half, nb)
@@ -279,25 +313,21 @@
     ).astype(F32)
     packed = a_full[...]
     scale = 2.0 * jnp.sum(packed * eye) / nb
-    y_re, y_im = halves(packed / scale)
-    y_re_b, y_im_b = y_re.astype(BF16), y_im.astype(BF16)
-    sq_re, sq_im = complex_mm(y_re_b, y_im_b, y_re_b, y_im_b)
-    left_re = (1.5 * y_re - 0.5 * sq_re).astype(BF16)
-    left_im = (1.5 * y_im - 0.5 * sq_im).astype(BF16)
-    right_re = (2.25 * eye - 1.5 * y_re + 0.25 * sq_re).astype(BF16)
-    right_im = (0.25 * sq_im - 1.5 * y_im).astype(BF16)
-    last_re, last_im = complex_mm(left_re, left_im, right_re, right_im)
-    white_re = 2.25 * eye - 0.75 * y_re - 0.5 * last_re
-    white_im = -0.75 * y_im - 0.5 * last_im
+    e_re, e_im = halves(packed / scale - 0.5 * eye)
+    e_re_b, e_im_b = e_re.astype(BF16), e_im.astype(BF16)
+    sq_re, sq_im = complex_mm(e_re_b, e_im_b, e_re_b, e_im_b)
+    left_re, left_im = e_re - 0.5 * sq_re, e_im - 0.5 * sq_im
+    right_re, right_im = 0.25 * sq_re - 1.25 * e_re, 0.25 * sq_im - 1.25 * e_im
+    last_re, last_im = complex_mm(
+        left_re.astype(BF16), left_im.astype(BF16), right_re.astype(BF16), right_im.astype(BF16)
+    )
+    white_re = 1.38671875 * eye - 0.75 * e_re - 0.78125 * left_re - 0.3125 * right_re - 0.5 * last_re
+    white_im = -0.75 * e_im - 0.78125 * left_im - 0.3125 * right_im - 0.5 * last_im
     w_buf[...] = (white_re + white_im).astype(BF16).reshape(CORES, half, nb)
     w_copies = to_near(w_buf.at[core], wn_buf.at[core], wn_recv.at[core], 2)
     for copy in w_copies:
         copy.start()
     w_re, w_im = white_re.astype(BF16), white_im.astype(BF16)
-
-    @pl.when(jnp.logical_not(outer))
-    def _():
-        over_pairs(reduce_one, pairs_a, pairs_all)
 
     out_re, out_im = complex_mm(f_buf[0], f_buf[1], w_re, w_im)
     white_out[0] = out_re.astype(BF16)
@@ -306,13 +336,15 @@
     v_buf[0] = v_re.astype(BF16)
     v_buf[1] = v_im.astype(BF16)
 
-    over_pairs(cast_one, pairs_a, pairs_all)
+    lax.fori_loop(early, pairs_all + CAST_LAG, sums, 0)
     from_near(un_buf, un_recv, 1)
     from_near(wn_buf, wn_recv, 2)
     next_re, next_im = halves(wn_buf[...].astype(F32).reshape(nb, nb))
     vn_re, vn_im = complex_mm(next_re.astype(BF16), next_im.astype(BF16), un_buf[0], un_buf[1])
-    cross_re = t_buf[A_CHUNKS : A_CHUNKS + c_chunks].reshape(nb, nb)
-    cross_im = t_buf[A_CHUNKS + c_chunks :].reshape(nb, nb)
+    cross_re, cross_im = (
+        jnp.concatenate([t_buf[A_CHUNKS + 2 * j + part] for j in range(c_chunks)], axis=0)
+        for part in range(2)
+    )
     x_re, x_im = complex_mm(cross_re, cross_im, vn_re.astype(BF16), vn_im.astype(BF16))
     x_re, x_im = x_re.astype(BF16), x_im.astype(BF16)
     root = math.sqrt(rows * pw_count)

time: 74.6 us -> 52.9 us (0.71)
  Pallas kernels: 69.1 us -> 47.4 us
    pallas_call x1, Pallas kernels: 69.1 us -> 47.4 us  [on_device(): pl.pallas_call(functools.partial(kernel, ka_count, pw_count), out_shape=(...]
where the time goes in v2:
time: 52.9 us; the launch traced here: 52.7 us
  Pallas kernels  47.4 us (90%)
  other arithmetic  3.3 us (6%)
  between operations  1.31 us (2%)
  local copies, waits for them, and re-layouts  0.68 us (1%)
    pallas_call x1, Pallas kernels, on_device(): pl.pallas_call(functools.partial(kernel, ka_count, pw_count), out_shape=(...  47.4 us
    broadcast_in_dim x1, other arithmetic, on_device(): return (whitened[None], correlations[None])  3.3 us

profile of v2, /device:TPU:0, one launch (start us, length us, event | category | flops | bytes accessed | tf_op | source)
XLA Modules:
  0.0 52.7 jit_solution(565356162843586162)
XLA Ops:
  1.3 47.4 %shard_map.68 = (bf16[2,128,384]{2,1,0:T(8,128)(2,1)}, bf16[2,2,384,384]{3,2,1,0:T(8,128)(2,1)}) custom-call(bf16[2,128,384]{2,1,0:T(8,128)(2,1)} %bitcast.12, f32[1,128]{1,0:T(1,128)} %weight_ref.1, s32[1,128]{1,0:T(1,128)} %order_ref.1, bf16[2,384,384]{2,1,0:T(8,128)(2,1)} %bitcast.10), custom_call_target="tpu_custom_call" | custom-call | tf_op jit(solution)/shard_map/pallas_call | solution.py:378
  48.7 0.0 copy-start
  48.7 3.3 %fusion.1 = f32[1,2,2,384,384]{4,3,2,1,0:T(8,128)} fusion(bf16[2,2,384,384]{3,2,1,0:T(8,128)(2,1)} %get-tuple-element.5, pred[]{:T(512)S(6)} %eq.5), kind=kLoop, calls=%fused_computation.2 | loop fusion | flops 1179648 | bytes 3538945 | tf_op jit(solution)/shard_map/broadcast_in_dim | solution.py:419
  52.0 0.0 copy-done
  52.1 0.7 %copy.9 = bf16[1,2,128,384]{3,2,1,0:T(8,128)(2,1)} copy(bf16[1,2,128,384]{3,2,1,0:T(8,128)(2,1)S(1)} %bitcast.11) | data formatting | bytes 393216
Async XLA Ops:
  48.7 3.3 %copy-start = (bf16[2,128,384]{2,1,0:T(8,128)(2,1)S(1)}, bf16[2,128,384]{2,1,0:T(8,128)(2,1)}, u32[]{:S(2)}) copy-start(bf16[2,128,384]{2,1,0:T(8,128)(2,1)} %get-tuple-element.4) | copy-start | bytes 589828

commit v3 on v2

--- a/solution.py
+++ b/solution.py
@@ -11,7 +11,8 @@
 MESH = pl.DeviceIdType.MESH
 CORES = 2
 A_CHUNKS = 4
-EARLY = 1
+EARLY = 3
+LATE = 3
 TOTAL_LAG = 3
 CAST_LAG = 6
 F32 = jnp.float32
@@ -109,6 +110,12 @@
     def _():
         greet(k, p + CORES)
 
+    eye = (
+        lax.broadcasted_iota(jnp.int32, (nb, nb), 0) == lax.broadcasted_iota(jnp.int32, (nb, nb), 1)
+    ).astype(F32)
+    first = lax.broadcasted_iota(jnp.int32, (nb, nb), 0) == 0
+    rest = jnp.where(first, 0.0, eye)
+
     row_id = lax.broadcasted_iota(jnp.int32, (rows, rows), 0)
     col_id = lax.broadcasted_iota(jnp.int32, (rows, rows), 1)
     weight = jnp.sum(jnp.where(row_id == col_id, weight_ref[...], 0.0), axis=1, keepdims=True)
@@ -151,8 +158,21 @@
     p_copy.start()
     f_copies = to_near(f_buf, fn_buf.at[core], fn_recv.at[core], 0)
     u_copies = to_near(gauge_ref.at[core], un_buf.at[core], un_recv.at[core], 1)
-    for copy in f_copies:
+    even = lax.rem(k, 2) == 0
+
+    @pl.when(even)
+    def _():
+        f_copies[1].start()
+        f_copies[0].start()
+
+    @pl.when(jnp.logical_not(even))
+    def _():
+        f_copies[0].start()
+        f_copies[1].start()
+
+    for copy in u_copies:
         copy.start()
+
 
     def got_pair(dst, turn):
         remote(dst, dst, pair_send.at[turn], pair_recv.at[turn], k, partner).wait_recv()
@@ -167,7 +187,8 @@
         return flat, jnp.concatenate(turned, axis=0)
 
     own_flat, own_turned = stacked(p_buf)
-    a_full[...] = mm_t(own_flat, own_flat) + mm_t(own_flat, own_turned)
+    gram = mm_t(own_flat, own_flat) + mm_t(own_flat, own_turned)
+    a_full[...] = gram - (jnp.sum(gram * eye) / nb) * rest
     for i in range(A_CHUNKS):
         local[i] = a_full[pl.ds(pl.multiple_of(core * half + i * chunk, 8), chunk), :]
 
@@ -281,9 +302,6 @@
     def _():
         cross_terms()
 
-    for copy in u_copies:
-        copy.start()
-
     def sums(j, carry):
         @pl.when(inner & (j < pairs_all))
         def _():
@@ -308,14 +326,13 @@
         a_other[...].astype(F32).reshape(half, nb)
     )
 
-    eye = (
-        lax.broadcasted_iota(jnp.int32, (nb, nb), 0) == lax.broadcasted_iota(jnp.int32, (nb, nb), 1)
-    ).astype(F32)
     packed = a_full[...]
-    scale = 2.0 * jnp.sum(packed * eye) / nb
-    e_re, e_im = halves(packed / scale - 0.5 * eye)
+    mean = jnp.sum(packed * eye)
+    deviation = packed - mean * (eye - rest)
+    e_re, e_im = halves(deviation / (2.0 * mean))
     e_re_b, e_im_b = e_re.astype(BF16), e_im.astype(BF16)
     sq_re, sq_im = complex_mm(e_re_b, e_im_b, e_re_b, e_im_b)
+    lax.fori_loop(early, early + 2, sums, 0)
     left_re, left_im = e_re - 0.5 * sq_re, e_im - 0.5 * sq_im
     right_re, right_im = 0.25 * sq_re - 1.25 * e_re, 0.25 * sq_im - 1.25 * e_im
     last_re, last_im = complex_mm(
@@ -329,6 +346,7 @@
         copy.start()
     w_re, w_im = white_re.astype(BF16), white_im.astype(BF16)
 
+    lax.fori_loop(early + 2, early + 5, sums, 0)
     out_re, out_im = complex_mm(f_buf[0], f_buf[1], w_re, w_im)
     white_out[0] = out_re.astype(BF16)
     white_out[1] = out_im.astype(BF16)
@@ -336,11 +354,12 @@
     v_buf[0] = v_re.astype(BF16)
     v_buf[1] = v_im.astype(BF16)
 
-    lax.fori_loop(early, pairs_all + CAST_LAG, sums, 0)
+    lax.fori_loop(early + 5, pairs_all + CAST_LAG - LATE, sums, 0)
     from_near(un_buf, un_recv, 1)
     from_near(wn_buf, wn_recv, 2)
     next_re, next_im = halves(wn_buf[...].astype(F32).reshape(nb, nb))
     vn_re, vn_im = complex_mm(next_re.astype(BF16), next_im.astype(BF16), un_buf[0], un_buf[1])
+    lax.fori_loop(pairs_all + CAST_LAG - LATE, pairs_all + CAST_LAG, sums, 0)
     cross_re, cross_im = (
         jnp.concatenate([t_buf[A_CHUNKS + 2 * j + part] for j in range(c_chunks)], axis=0)
         for part in range(2)
@@ -415,7 +434,9 @@
     )(band_coeffs[0], cutoff_weight, row_order, gauge_matrix[0])
     group = lax.axis_index("ka")
     looks_ahead = neighbour[0] == (group + 1) % ka_count
-    correlations = jnp.where(looks_ahead, pair, pair[::-1]).astype(F32)
+    correlations = jnp.stack(
+        [jnp.where(looks_ahead, pair[0], pair[1]), jnp.where(looks_ahead, pair[1], pair[0])]
+    ).astype(F32)
     return (whitened[None], correlations[None])
 
 

time: 52.9 us -> 49.7 us (0.940)
  Pallas kernels: 47.4 us -> 44.7 us
    broadcast_in_dim x1 -> x0, other arithmetic: 3.3 us -> none  [on_device(): return (whitened[None], correlations[None])]
    pallas_call x1, Pallas kernels: 47.4 us -> 44.7 us  [on_device(): pl.pallas_call(functools.partial(kernel, ka_count, pw_count), out_shape=(...]
    convert_element_type x0 -> x1, other arithmetic: none -> 1.56 us  [on_device(): correlations = jnp.stack([jnp.where(looks_ahead, pair[0], pair[1]), jnp.w...]
    another operation x0 -> x1, other arithmetic: none -> 1.36 us  [on_device(): jnp.stack([jnp.where(looks_ahead, pair[0], pair[1]), jnp.where(looks_ahea...]
where the time goes in v3:
time: 49.7 us; the launch traced here: 49.6 us
  Pallas kernels  44.7 us (90%)
  other arithmetic  2.92 us (6%)
  between operations  1.31 us (3%)
  local copies, waits for them, and re-layouts  0.68 us (1%)
    pallas_call x1, Pallas kernels, on_device(): pl.pallas_call(functools.partial(kernel, ka_count, pw_count), out_shape=(...  44.7 us
    convert_element_type x1, other arithmetic, on_device(): correlations = jnp.stack([jnp.where(looks_ahead, pair[0], pair[1]), jnp.w...  1.56 us
    another operation x1, other arithmetic, on_device(): jnp.stack([jnp.where(looks_ahead, pair[0], pair[1]), jnp.where(looks_ahea...  1.36 us

profile of v3, /device:TPU:0, one launch (start us, length us, event | category | flops | bytes accessed | tf_op | source)
XLA Modules:
  0.0 49.6 jit_solution(9482282656551894965)
XLA Ops:
  1.3 44.7 %shard_map.68 = (bf16[2,128,384]{2,1,0:T(8,128)(2,1)}, bf16[2,2,384,384]{3,2,1,0:T(8,128)(2,1)}) custom-call(bf16[2,128,384]{2,1,0:T(8,128)(2,1)} %bitcast.11, f32[1,128]{1,0:T(1,128)} %weight_ref.1, s32[1,128]{1,0:T(1,128)} %order_ref.1, bf16[2,384,384]{2,1,0:T(8,128)(2,1)} %bitcast.9), custom_call_target="tpu_custom_call" | custom-call | tf_op jit(solution)/shard_map/pallas_call | solution.py:397
  46.0 1.4 %select_bitcast_fusion.1 = (bf16[1,1,2,384,384]{4,3,2,1,0:T(8,128)(2,1)S(1)}, bf16[1,1,2,384,384]{4,3,2,1,0:T(8,128)(2,1)S(1)}) fusion(pred[]{:T(512)S(6)} %eq.5, bf16[2,2,384,384]{3,2,1,0:T(8,128)(2,1)} %get-tuple-element.5), kind=kLoop, calls=%fused_computation.2 | loop fusion | flops 589824 | bytes 2359297 | tf_op jit(solution)/shard_map/stack | solution.py:437
  47.3 0.0 copy-start
  47.3 1.6 %maximum_convert_fusion = f32[1,2,2,384,384]{4,3,2,1,0:T(8,128)} fusion(bf16[1,1,2,384,384]{4,3,2,1,0:T(8,128)(2,1)S(1)} %get-tuple-element.7, bf16[1,1,2,384,384]{4,3,2,1,0:T(8,128)(2,1)S(1)} %get-tuple-element.6), kind=kLoop, calls=%fused_computation | loop fusion | flops 1179648 | bytes 3538944 | tf_op jit(solution)/shard_map/convert_element_type | solution.py:439
  48.9 0.0 copy-done
  48.9 0.7 %copy.9 = bf16[1,2,128,384]{3,2,1,0:T(8,128)(2,1)} copy(bf16[1,2,128,384]{3,2,1,0:T(8,128)(2,1)S(1)} %bitcast.10) | data formatting | bytes 393216
Async XLA Ops:
  47.3 1.6 %copy-start = (bf16[2,128,384]{2,1,0:T(8,128)(2,1)S(1)}, bf16[2,128,384]{2,1,0:T(8,128)(2,1)}, u32[]{:S(2)}) copy-start(bf16[2,128,384]{2,1,0:T(8,128)(2,1)} %get-tuple-element.4) | copy-start | bytes 589828
